TPU v7x, 256 devices: a whole 4x4x8 slice. The times are simulated.
256 devices in a mesh: group: 32 (over z, x_lo, core), rep: 8 (over x_hi, y).
Axes of the slice: x: 4 (x_hi: 2, x_lo: 2; x = x_hi * 2 + x_lo), y: 4, z: 8, core: 2. Of those that a mesh axis runs over, the one named last changes fastest.
Arguments:
- queries: bfloat16 [256, 256, 3072], P(('group', 'rep')), may hold values from -46 to 46
- keys: bfloat16 [256, 256, 3072], P(('group', 'rep')), may hold values from -46 to 46
- values: bfloat16 [256, 256, 3072], P(('group', 'rep')), may hold values from -24 to 24
- grad_output: bfloat16 [256, 256, 3072], P(('group', 'rep')), may hold values from -6 to 6
- weight_codes: bfloat16 [3072, 3072], P('group'), may hold values from -4 to 4
- weight_scales: float32 [3072, 12], P('group'), may hold values from 0.006 to 0.06
Outputs:
- grad_queries: bfloat16 [256, 256, 3072], P(('group', 'rep'))
- grad_keys: bfloat16 [256, 256, 3072], P(('group', 'rep'))
- grad_values: bfloat16 [256, 256, 3072], P(('group', 'rep'))
- grad_weight: float32 [3072, 3072], P(('group', 'rep'))
All inputs are finite; a program needn't handle non-finite values.
Results may differ from a plain program's by a relative error of at most 0.029.
Values may be sent and summed in bfloat16 or wider, within the bound.
No kernel may reach another device: no remote copies, remote signals or barrier semaphores. Data moves between devices by JAX's collectives and lax.ppermute only.
A program may use at most 128 MiB of HBM per device.

v0:
```python
import jax
import jax.numpy as jnp
from jax import lax
from jax.sharding import Mesh
from jax.sharding import PartitionSpec as P

HD = 128
GROUP = ("group_0", "group_1", "group_2")
GROUP_REP = ("group_0", "group_1", "group_2", "rep")


def from_everyone(value, axis):
    count = lax.axis_size(axis)
    return lax.all_to_all(
        jnp.broadcast_to(value[None], (count, *value.shape)), axis, 0, 0, tiled=True
    )


def in_order(pieces, dim):
    shape = list(pieces.shape[1:])
    shape[dim] *= pieces.shape[0]
    return jnp.moveaxis(pieces, 0, dim).reshape(shape)


def gather_axes(value, axes, dim):
    far, near = axes
    pieces = from_everyone(from_everyone(value, far), near)
    return in_order(pieces.swapaxes(0, 1).reshape(-1, *value.shape), dim)


def cut_along(value, dim, count):
    before, after = (value.shape[:dim], value.shape[dim + 1 :])
    return jnp.moveaxis(value.reshape(*before, count, -1, *after), dim, 0)


def sent_and_summed(value, axis, dim):
    count = lax.axis_size(axis)
    pieces = lax.all_to_all(cut_along(value, dim, count), axis, 0, 0, tiled=True)
    return jnp.sum(pieces, axis=0)


def sum_in_two_steps(value, axes, dim):
    far, near = axes
    pieces = cut_along(value, dim, lax.axis_size(far))
    nearer = sent_and_summed(pieces, near, dim + 1)
    arrived = lax.all_to_all(nearer, far, split_axis=0, concat_axis=0, tiled=True)
    return arrived.sum(axis=0)


def restore(code_rows, scale_rows):
    row_count = code_rows.shape[0]
    block_count = scale_rows.shape[1]
    spread = (
        code_rows.astype(jnp.float32).reshape(row_count, block_count, -1) * scale_rows[:, :, None]
    )
    return spread.reshape(row_count, -1).astype(jnp.bfloat16)


def forward_image(arrays_in):
    query, keyset, valueset = arrays_in
    seq_len = query.shape[0]
    head_count = query.shape[1] // HD
    query_heads = query.reshape(seq_len, head_count, HD)
    key_heads = keyset.reshape(seq_len, head_count, HD)
    value_heads = valueset.reshape(seq_len, head_count, HD)
    scores = jnp.einsum(
        "qhd,khd->hqk", query_heads, key_heads, preferred_element_type=jnp.float32
    ) * HD ** (-0.5)
    highest = jnp.max(scores, axis=2, keepdims=True)
    exponent = jnp.exp(scores - highest)
    probability = exponent / jnp.sum(exponent, axis=2, keepdims=True)
    weight_half = probability.astype(jnp.bfloat16)
    context = jnp.einsum(
        "hqk,khd->qhd", weight_half, value_heads, preferred_element_type=jnp.float32
    )
    return (probability, context.astype(jnp.bfloat16).reshape(seq_len, -1))


def backward_image(arrays_in):
    query, keyset, valueset, probability, grad_context = arrays_in
    seq_len = query.shape[0]
    head_count = query.shape[1] // HD
    query_heads = query.reshape(seq_len, head_count, HD)
    key_heads = keyset.reshape(seq_len, head_count, HD)
    value_heads = valueset.reshape(seq_len, head_count, HD)
    grad_heads = grad_context.reshape(seq_len, head_count, HD)
    weight_half = probability.astype(jnp.bfloat16)
    grad_value = jnp.einsum(
        "hqk,qhd->khd", weight_half, grad_heads, preferred_element_type=jnp.float32
    )
    dprobs = jnp.einsum("qhd,khd->hqk", grad_heads, value_heads, preferred_element_type=jnp.float32)
    row_delta = jnp.sum(probability * dprobs, axis=2, keepdims=True)
    dscores = (probability * (dprobs - row_delta) * HD ** (-0.5)).astype(jnp.bfloat16)
    grad_query = jnp.einsum("hqk,khd->qhd", dscores, key_heads, preferred_element_type=jnp.float32)
    grad_key = jnp.einsum("hqk,qhd->khd", dscores, query_heads, preferred_element_type=jnp.float32)
    return (
        grad_query.astype(jnp.bfloat16).reshape(seq_len, -1),
        grad_key.astype(jnp.bfloat16).reshape(seq_len, -1),
        grad_value.astype(jnp.bfloat16).reshape(seq_len, -1),
    )


def per_device(queries, keys, values, grad_output, weight_codes, weight_scales):
    image_count, seq_len, row_total = queries.shape
    feature_count = grad_output.shape[2]
    local_rows = image_count * seq_len
    probability, contexts = lax.map(forward_image, (queries, keys, values))
    context_flat = contexts.reshape(local_rows, row_total)
    output_flat = grad_output.reshape(local_rows, feature_count)
    group_count = lax.axis_size(GROUP)
    replica_count = lax.axis_size("rep")
    slab_rows = row_total // (group_count * replica_count)
    first_row = lax.axis_index("rep") * slab_rows
    codes_part = lax.dynamic_slice_in_dim(weight_codes, first_row, slab_rows, 0)
    scales_part = lax.dynamic_slice_in_dim(weight_scales, first_row, slab_rows, 0)
    all_output = lax.all_gather(output_flat, "rep", axis=0, tiled=True)
    split_context = jnp.moveaxis(
        context_flat.reshape(local_rows, group_count, replica_count, slab_rows), 2, 0
    )
    split_context = split_context.reshape(replica_count, local_rows, group_count * slab_rows)
    gathered_ctx = lax.all_to_all(split_context, "rep", split_axis=0, concat_axis=1, tiled=True)
    gathered_ctx = gathered_ctx.reshape(replica_count, local_rows, group_count * slab_rows)
    grad_columns = jnp.dot(
        all_output,
        restore(
            gather_axes(codes_part, (("group_0", "group_1"), "group_2"), 0),
            gather_axes(
                scales_part.astype(jnp.bfloat16), (("group_0", "group_1"), "group_2"), 0
            ).astype(scales_part.dtype),
        ).T,
        preferred_element_type=jnp.float32,
    ).astype(jnp.bfloat16)
    output_blocks = all_output.reshape(replica_count, local_rows, feature_count)
    device_terms = jnp.einsum(
        "rlp,rle->rpe", gathered_ctx, output_blocks, preferred_element_type=jnp.float32
    ).astype(jnp.bfloat16)
    grad_weight = sum_in_two_steps(
        jnp.sum(lax.optimization_barrier(device_terms).astype(jnp.float32), axis=0),
        (("group_0", "group_1"), "group_2"),
        0,
    )
    returned = lax.all_to_all(
        grad_columns.reshape(1, replica_count * local_rows, group_count * slab_rows),
        "rep",
        split_axis=1,
        concat_axis=0,
        tiled=True,
    )
    returned = jnp.moveaxis(
        returned.reshape(replica_count, local_rows, group_count, slab_rows), 0, 2
    )
    grad_context = returned.reshape(image_count, seq_len, row_total)
    grad_queries, grad_keys, grad_values = lax.map(
        backward_image, (queries, keys, values, probability, grad_context)
    )
    return (grad_queries, grad_keys, grad_values, grad_weight)


def solution(mesh):
    split = Mesh(
        mesh.devices.reshape(8, 2, 2, mesh.shape["rep"]), ("group_0", "group_1", "group_2", "rep")
    )
    return jax.shard_map(
        per_device,
        mesh=split,
        in_specs=(
            P(GROUP_REP, None, None),
            P(GROUP_REP, None, None),
            P(GROUP_REP, None, None),
            P(GROUP_REP, None, None),
            P(GROUP, None),
            P(GROUP, None),
        ),
        out_specs=(
            P(GROUP_REP, None, None),
            P(GROUP_REP, None, None),
            P(GROUP_REP, None, None),
            P(GROUP_REP, None),
        ),
        check_vma=False,
    )
```

profile of v0, /device:TPU:4, one launch (start us, length us, event | category | flops | bytes accessed | tf_op | source)
XLA Modules:
  0.0 398.7 jit_solution(12941961424991909647)
XLA Ops:
  7.2 0.0 copy-start
  7.2 0.0 all-gather.3.cloned.1.call-start
  7.2 0.7 all-gather.3.cloned.1.call-update
  7.9 0.9 dynamic-slice_convert_fusion
  8.8 0.6 broadcast_in_dim.52
  9.5 9.2 %all-to-all-start.2 = ((bf16[16,12,12]{1,2,0:T(8,128)(2,1)}), bf16[16,12,12]{1,2,0:T(8,128)(2,1)S(1)}, u32[]{:S(2)}, u32[]{:S(2)}) async-start(bf16[16,12,12]{1,2,0:T(8,128)(2,1)} %broadcast_in_dim.52), calls=%async_computation.2 | async-start | bytes 131072 | tf_op jit(solution)/shard_map/all_to_all | solution.py:14
  18.7 9.0 %all-to-all-done.2 = bf16[16,12,12]{1,2,0:T(8,128)(2,1)S(1)} async-done(((bf16[16,12,12]{1,2,0:T(8,128)(2,1)}), bf16[16,12,12]{1,2,0:T(8,128)(2,1)S(1)}, u32[]{:S(2)}, u32[]{:S(2)}) %all-to-all-start.2) | async-done | bytes 4640 | tf_op jit(solution)/shard_map/all_to_all | solution.py:14
  27.8 0.2 reshape.109
  27.9 3.7 all_to_all.48
  31.6 1.3 broadcast_in_dim.50
  33.0 4.4 %all-to-all-start = ((bf16[16,12,3072]{2,1,0:T(8,128)(2,1)}), bf16[16,12,3072]{2,1,0:T(8,128)(2,1)}, u32[]{:S(2)}, u32[]{:S(2)}) async-start(bf16[16,12,3072]{2,1,0:T(8,128)(2,1)} %broadcast_in_dim.50), calls=%async_computation | async-start | bytes 3145728 | tf_op jit(solution)/shard_map/all_to_all | solution.py:14
  37.4 1.6 copy.148
  39.0 2.6 copy.147
  41.6 1.7 copy.149
  43.3 0.0 copy-start.3
  43.3 7.4 %fusion.43 = (f32[24,256]{1,0:T(8,128)S(1)}, f32[24,256,256]{1,2,0:T(8,128)}) fusion(bf16[256,24,128]{0,2,1:T(8,128)(2,1)} %bitcast.77, bf16[256,24,128]{0,2,1:T(8,128)(2,1)} %bitcast.79), kind=kOutput, calls=%fused_computation.38 | convolution fusion | flops 407372032 | bytes 9461760 | tf_op jit(solution)/shard_map/while/body/eval_jaxpr/sub | solution.py:70
  50.7 4.6 %fusion.33 = bf16[256,24,128]{0,2,1:T(8,128)(2,1)} fusion(bf16[256,24,128]{0,2,1:T(8,128)(2,1)S(1)} %bitcast.72, f32[24,256,256]{1,2,0:T(8,128)} %get-tuple-element.74, f32[24,256]{1,0:T(8,128)S(1)} %get-tuple-element.73), kind=kOutput, calls=%fused_computation.28 | convolution fusion | flops 406585344 | bytes 9461760 | tf_op jit(solution)/shard_map/while/body/eval_jaxpr/hqk,khd->qhd/dot_general | solution.py:73
  55.3 2.4 reshape_reshape.8
  57.6 0.7 copy.135
  58.4 1.5 copy.136
  59.8 0.2 reshape.110
  60.1 0.2 copy.121
  60.2 0.3 reshape.106
  60.5 2.4 mul.32
  63.0 6.1 %copy.122 = f32[384,3072]{1,0:T(8,128)} copy(f32[384,3072]{0,1:T(8,128)} %bitcast.67) | data formatting | bytes 9437184 | tf_op jit(solution)/shard_map/mul | solution.py:54
  69.0 8.3 %all-to-all-done = bf16[16,12,3072]{2,1,0:T(8,128)(2,1)} async-done(((bf16[16,12,3072]{2,1,0:T(8,128)(2,1)}), bf16[16,12,3072]{2,1,0:T(8,128)(2,1)}, u32[]{:S(2)}, u32[]{:S(2)}) %all-to-all-start) | async-done | bytes 1179680 | tf_op jit(solution)/shard_map/all_to_all | solution.py:14
  77.3 2.1 copy.118
  79.4 0.3 broadcast_in_dim.51
  79.7 5.6 %all_to_all.49 = bf16[2,16,12,3072]{3,1,2,0:T(8,128)(2,1)S(1)} all-to-all(bf16[2,16,12,3072]{3,1,2,0:T(8,128)(2,1)S(1)} %broadcast_in_dim.51), channel_id=1, replica_groups=mesh['group_0'=8,'group_1'=2,'group_2'=2,'rep'=8] {'group_2'}, dimensions={0} | all-to-all | bytes 4718592 | tf_op jit(solution)/shard_map/all_to_all | solution.py:14
  85.3 8.0 %all-to-all-start.5 = ((bf16[8,256,384]{1,2,0:T(8,128)(2,1)}), bf16[8,256,384]{1,2,0:T(8,128)(2,1)}, u32[]{:S(2)}, u32[]{:S(2)}) async-start(bf16[8,256,384]{1,2,0:T(8,128)(2,1)} %copy.136), calls=%async_computation.5 | async-start | bytes 3145728 | tf_op jit(solution)/shard_map/all_to_all | solution.py:121
  93.3 0.6 convert_bitcast_fusion
  93.8 5.5 %copy.119 = f32[16,2,12,3072]{3,2,1,0:T(8,128)} copy(f32[16,2,12,3072]{3,0,2,1:T(8,128)S(1)} %convert_bitcast_fusion) | data formatting | bytes 9437184 | tf_op jit(solution)/shard_map/convert_element_type | solution.py:54
  99.3 5.4 %reshape.105 = f32[384,3072]{1,0:T(8,128)} reshape(f32[16,2,12,3072]{3,2,1,0:T(8,128)} %copy.119) | data formatting | bytes 9437184 | tf_op jit(solution)/shard_map/convert_element_type | solution.py:54
  104.8 77.1 %all-gather.3.cloned.1.call-done = bf16[1,2048,3072]{2,1,0:T(8,128)(2,1)} async-done(((bf16[1,256,3072]{2,1,0:T(8,128)(2,1)}), bf16[1,2048,3072]{2,1,0:T(8,128)(2,1)}) %all-gather.3.cloned.1.call-update) | async-done | bytes 12582928 | tf_op jit(solution)/shard_map/all_gather | solution.py:116
  181.9 10.8 %fusion.22 = bf16[1,2048,384]{1,2,0:T(8,128)(2,1)S(1)} fusion(bf16[1,2048,3072]{2,1,0:T(8,128)(2,1)} %all-gather.3.cloned.1.call-done, f32[384,3072]{1,0:T(8,128)} %reshape.105, f32[384,3072]{1,0:T(8,128)} %copy.122), kind=kOutput, calls=%fused_computation.21 | convolution fusion | flops 4834983936 | bytes 23592960 | tf_op jit(solution)/shard_map/dot_general | solution.py:123
  192.7 5.6 %copy.123 = bf16[1,2048,384]{2,0,1:T(2,128)(2,1)} copy(bf16[1,2048,384]{1,2,0:T(8,128)(2,1)S(1)} %fusion.22) | data formatting | bytes 3145728 | tf_op jit(solution)/shard_map/reshape | solution.py:143
  198.3 0.5 broadcast.35
  198.9 34.3 %reduce = bf16[2048,384]{1,0:T(8,128)(2,1)S(1)} reduce(bf16[2048,1,384]{2,1,0:T(2,128)(2,1)} %bitcast.68, bf16[]{:T(256)} %broadcast.35), dimensions={1}, to_apply=%bitcast.50.reduce_sub_computation | reduce | bytes 3145730
  233.2 1.9 reshape.111
  235.0 0.0 all-to-all-done.5
  235.0 14.1 %convolution_convert_fusion = bf16[8,384,3072]{2,1,0:T(8,128)(2,1)} fusion(bf16[8,256,384]{1,2,0:T(8,128)(2,1)} %all-to-all-done.5, bf16[8,256,3072]{2,1,0:T(8,128)(2,1)} %bitcast.70), kind=kOutput, calls=%fused_computation.5 | convolution fusion | flops 4841275392 | bytes 33030144 | tf_op jit(solution)/shard_map/rlp,rle->rpe/dot_general | solution.py:134
  249.1 12.8 %convert_reduce_fusion = f32[384,3072]{1,0:T(8,128)} fusion(bf16[8,384,3072]{2,1,0:T(8,128)(2,1)} %convolution_convert_fusion), kind=kLoop, calls=%fused_computation.2 | loop fusion | flops 17694720 | bytes 23592960 | tf_op jit(solution)/shard_map/reduce_sum | solution.py:138
  261.9 5.5 %reshape_reshape.9 = f32[16,2,12,3072]{3,2,1,0:T(8,128)} reshape(f32[384,3072]{1,0:T(8,128)} %convert_reduce_fusion) | data formatting | bytes 9437184 | tf_op jit(solution)/shard_map/reshape;reshape | solution.py:33
  267.4 5.5 %copy.137 = f32[2,16,12,3072]{3,1,2,0:T(8,128)S(1)} copy(f32[2,16,12,3072]{3,2,0,1:T(8,128)} %bitcast.66) | data formatting | bytes 9437184 | tf_op jit(solution)/shard_map/transpose | solution.py:33
  272.9 8.6 %all_to_all.50 = f32[2,16,12,3072]{3,1,2,0:T(8,128)} all-to-all(f32[2,16,12,3072]{3,1,2,0:T(8,128)S(1)} %copy.137), channel_id=1, replica_groups=mesh['group_0'=8,'group_1'=2,'group_2'=2,'rep'=8] {'group_2'}, dimensions={0} | all-to-all | bytes 9437184 | tf_op jit(solution)/shard_map/all_to_all | solution.py:38
  281.6 6.9 %all-to-all-start.4 = ((bf16[8,2,49152]{2,1,0:T(2,128)(2,1)}), bf16[8,2,49152]{2,1,0:T(2,128)(2,1)}, u32[]{:S(2)}, u32[]{:S(2)}) async-start(bf16[8,2,49152]{2,1,0:T(2,128)(2,1)} %reshape.111), calls=%async_computation.4 | async-start | bytes 3145728 | tf_op jit(solution)/shard_map/all_to_all | solution.py:142
  288.5 2.9 reduce_sum.50
  291.4 3.0 copy.138
  294.4 14.6 %all-to-all-done.4 = bf16[8,2,49152]{2,1,0:T(2,128)(2,1)} async-done(((bf16[8,2,49152]{2,1,0:T(2,128)(2,1)}), bf16[8,2,49152]{2,1,0:T(2,128)(2,1)}, u32[]{:S(2)}, u32[]{:S(2)}) %all-to-all-start.4) | async-done | bytes 1572896 | tf_op jit(solution)/shard_map/all_to_all | solution.py:142
  309.0 6.4 %all-to-all-start.7 = ((f32[16,12,3072]{2,1,0:T(8,128)}), f32[16,12,3072]{2,1,0:T(8,128)}, u32[]{:S(2)}, u32[]{:S(2)}) async-start(f32[16,12,3072]{2,1,0:T(8,128)} %copy.138), calls=%async_computation.7 | async-start | bytes 6291456 | tf_op jit(solution)/shard_map/all_to_all | solution.py:46
  315.5 6.3 %reshape.112 = bf16[2048,1,384]{2,1,0:T(2,128)(2,1)} reshape(bf16[8,2,49152]{2,1,0:T(2,128)(2,1)} %all-to-all-done.4) | data formatting | bytes 3145728
  321.8 6.8 %copy.124 = bf16[1,2048,384]{1,2,0:T(8,128)(2,1)S(1)} copy(bf16[1,2048,384]{2,0,1:T(2,128)(2,1)} %bitcast.69) | data formatting | bytes 3145728 | tf_op jit(solution)/shard_map/all_to_all | solution.py:142
  328.6 0.5 copy.150
  329.1 0.5 copy.125
  329.6 1.3 reshape.101
  331.0 5.6 %convolution_convert_fusion.2 = bf16[24,128,256]{2,1,0:T(8,128)(2,1)} fusion(bf16[256,24,128]{0,2,1:T(8,128)(2,1)} %reshape.101, f32[24,256,256]{1,2,0:T(8,128)} %get-tuple-element.74, f32[24,256]{1,0:T(8,128)S(1)} %get-tuple-element.73), kind=kOutput, calls=%fused_computation.25 | convolution fusion | flops 406585344 | bytes 9461760 | tf_op jit(solution)/shard_map/while/body/eval_jaxpr/hqk,qhd->khd/dot_general | solution.py:88
  336.6 2.7 copy.141
  339.3 5.1 %fusion.44 = f32[24,256,256]{1,2,0:T(8,128)} fusion(bf16[256,24,128]{0,2,1:T(8,128)(2,1)} %bitcast.73, bf16[256,24,128]{0,2,1:T(8,128)(2,1)S(1)} %copy-done.2), kind=kOutput, calls=%fused_computation.40 | convolution fusion | flops 402653184 | bytes 9437184 | tf_op jit(solution)/shard_map/while/body/eval_jaxpr/qhd,khd->hqk/dot_general | solution.py:91
  344.3 12.2 %fusion.25 = bf16[24,256,128]{1,2,0:T(8,128)(2,1)} fusion(bf16[256,24,128]{0,2,1:T(8,128)(2,1)} %bitcast.80, f32[24,256,256]{1,2,0:T(8,128)} %fusion.44, f32[24,256,256]{1,2,0:T(8,128)} %get-tuple-element.74, f32[24,256]{1,0:T(8,128)S(1)} %get-tuple-element.73), kind=kOutput, calls=%fused_computation.22 | convolution fusion | flops 414456064 | bytes 15753216 | tf_op jit(solution)/shard_map/while/body/eval_jaxpr/hqk,khd->qhd/dot_general | solution.py:94
  356.5 2.7 copy.139
  359.2 11.9 %fusion.28 = bf16[24,256,128]{1,2,0:T(8,128)(2,1)} fusion(bf16[256,24,128]{0,2,1:T(8,128)(2,1)S(1)} %bitcast.78, f32[24,256,256]{1,2,0:T(8,128)} %fusion.44, f32[24,256,256]{1,2,0:T(8,128)} %get-tuple-element.74, f32[24,256]{1,0:T(8,128)S(1)} %get-tuple-element.73), kind=kOutput, calls=%fused_computation.23 | convolution fusion | flops 414456064 | bytes 15753216 | tf_op jit(solution)/shard_map/while/body/eval_jaxpr/hqk,qhd->khd/dot_general | solution.py:95
  371.1 2.6 copy.140
  373.8 15.1 %all-to-all-done.7 = f32[16,12,3072]{2,1,0:T(8,128)} async-done(((f32[16,12,3072]{2,1,0:T(8,128)}), f32[16,12,3072]{2,1,0:T(8,128)}, u32[]{:S(2)}, u32[]{:S(2)}) %all-to-all-start.7) | async-done | bytes 2359328 | tf_op jit(solution)/shard_map/all_to_all | solution.py:46
  388.8 2.8 reduce_sum.51
  (14 shorter events, 0.1 us)
Async XLA Ops:
  7.2 11.5 %copy-start = (bf16[96,3072]{1,0:T(8,128)(2,1)S(1)}, bf16[96,3072]{1,0:T(8,128)(2,1)}, u32[]{:S(2)}) copy-start(bf16[96,3072]{1,0:T(8,128)(2,1)} %param.10) | copy-start | bytes 1769476
  7.2 174.7 %all-gather.3.cloned.1.call-start = ((), (), s32[]{:S(2)}) async-start(), calls=%async_computation.8 | async-start | bytes 14155776 | tf_op jit(solution)/shard_map/all_gather | solution.py:116
  7.9 29.5 %copy-start.4 = (bf16[1,256,3072]{2,1,0:T(8,128)(2,1)S(1)}, bf16[1,256,3072]{2,1,0:T(8,128)(2,1)}, u32[]{:S(2)}) copy-start(bf16[1,256,3072]{2,1,0:T(8,128)(2,1)} %param.6) | copy-start | bytes 4718596
  9.5 18.3 %all-to-all-start.2 = ((bf16[16,12,12]{1,2,0:T(8,128)(2,1)}), bf16[16,12,12]{1,2,0:T(8,128)(2,1)S(1)}, u32[]{:S(2)}, u32[]{:S(2)}) async-start(bf16[16,12,12]{1,2,0:T(8,128)(2,1)} %broadcast_in_dim.52), calls=%async_computation.2 | async-start | bytes 131072 | tf_op jit(solution)/shard_map/all_to_all | solution.py:14
  33.0 44.4 %all-to-all-start = ((bf16[16,12,3072]{2,1,0:T(8,128)(2,1)}), bf16[16,12,3072]{2,1,0:T(8,128)(2,1)}, u32[]{:S(2)}, u32[]{:S(2)}) async-start(bf16[16,12,3072]{2,1,0:T(8,128)(2,1)} %broadcast_in_dim.50), calls=%async_computation | async-start | bytes 3145728 | tf_op jit(solution)/shard_map/all_to_all | solution.py:14
  43.3 7.4 %copy-start.3 = (bf16[1,256,3072]{1,2,0:T(8,128)(2,1)}, bf16[1,256,3072]{1,2,0:T(8,128)(2,1)S(1)}, u32[]{:S(2)}) copy-start(bf16[1,256,3072]{1,2,0:T(8,128)(2,1)S(1)} %copy.149) | copy-start | bytes 4718596
  85.3 149.7 %all-to-all-start.5 = ((bf16[8,256,384]{1,2,0:T(8,128)(2,1)}), bf16[8,256,384]{1,2,0:T(8,128)(2,1)}, u32[]{:S(2)}, u32[]{:S(2)}) async-start(bf16[8,256,384]{1,2,0:T(8,128)(2,1)} %copy.136), calls=%async_computation.5 | async-start | bytes 3145728 | tf_op jit(solution)/shard_map/all_to_all | solution.py:121
  281.6 27.5 %all-to-all-start.4 = ((bf16[8,2,49152]{2,1,0:T(2,128)(2,1)}), bf16[8,2,49152]{2,1,0:T(2,128)(2,1)}, u32[]{:S(2)}, u32[]{:S(2)}) async-start(bf16[8,2,49152]{2,1,0:T(2,128)(2,1)} %reshape.111), calls=%async_computation.4 | async-start | bytes 3145728 | tf_op jit(solution)/shard_map/all_to_all | solution.py:142
  309.0 79.8 %all-to-all-start.7 = ((f32[16,12,3072]{2,1,0:T(8,128)}), f32[16,12,3072]{2,1,0:T(8,128)}, u32[]{:S(2)}, u32[]{:S(2)}) async-start(f32[16,12,3072]{2,1,0:T(8,128)} %copy.138), calls=%async_computation.7 | async-start | bytes 6291456 | tf_op jit(solution)/shard_map/all_to_all | solution.py:46
  336.6 2.7 copy-start.2
  356.5 2.7 copy-start.5
  371.1 20.5 %copy-start.1 = (bf16[96,3072]{1,0:T(8,128)(2,1)S(1)}, bf16[96,3072]{1,0:T(8,128)(2,1)}, u32[]{:S(2)}) copy-start(bf16[96,3072]{1,0:T(8,128)(2,1)} %param.10) | copy-start | bytes 1769476
Sparse Core Ops, SparseCore 0:
  10.6 171.2 all-gather.2
where the time goes:
time: 406 us; the launch traced here: 399 us
  waiting for transfers between devices  125 us (31%)
  local copies, waits for them, and re-layouts  81.5 us (20%)
  matrix products  71.7 us (18%)
  other arithmetic  53.3 us (13%)
  starting transfers between devices  35 us (9%)
  blocking collectives  18 us (4%)
  between operations  14.5 us (4%)
    all_gather x1, waiting for transfers between devices, per_device(): all_output = lax.all_gather(output_flat, 'rep', axis=0, tiled=True)  77.1 us
    unnamed x1, other arithmetic  34.3 us
    unnamed x22, local copies, waits for them, and re-layouts  17.7 us
    all_to_all x2, waiting for transfers between devices, from_everyone(): lax.all_to_all(jnp.broadcast_to(value[None], (count, *value.shape)), axis...  17.3 us
    all_to_all x1, waiting for transfers between devices, sum_in_two_steps(): lax.all_to_all(nearer, far, split_axis=0, concat_axis=0, tiled=True)  15.1 us
    all_to_all x1, waiting for transfers between devices, per_device(): lax.all_to_all(grad_columns.reshape(1, replica_count * local_rows, group_...  14.6 us
    dot_general x1, matrix products, per_device(): jnp.einsum('rlp,rle->rpe', gathered_ctx, output_blocks, preferred_element...  14.1 us
    all_to_all x2, starting transfers between devices, from_everyone(): lax.all_to_all(jnp.broadcast_to(value[None], (count, *value.shape)), axis...  13.6 us
  transfers between devices with their start and end apart: 6, of which 5 were waited for; matrix products, arithmetic and copies ran while one was open for 42% of the time, Pallas kernels for 0%

commit v1 on v0

--- a/solution.py
+++ b/solution.py
@@ -139,12 +139,20 @@
         (("group_0", "group_1"), "group_2"),
         0,
     )
-    returned = lax.all_to_all(
-        grad_columns.reshape(1, replica_count * local_rows, group_count * slab_rows),
-        "rep",
-        split_axis=1,
-        concat_axis=0,
-        tiled=True,
+    returned = jnp.concatenate(
+        lax.all_to_all(
+            jnp.stack(
+                jnp.split(
+                    grad_columns.reshape(1, replica_count * local_rows, group_count * slab_rows),
+                    lax.axis_size("rep"),
+                    axis=1,
+                )
+            ),
+            "rep",
+            0,
+            0,
+        ),
+        axis=0,
     )
     returned = jnp.moveaxis(
         returned.reshape(replica_count, local_rows, group_count, slab_rows), 0, 2

time: 406 us -> 363 us (0.89); the launches traced: 399 us -> 361 us
  other arithmetic: 53.3 us -> 19 us
  local copies, waits for them, and re-layouts: 81.5 us -> 67.7 us
  waiting for transfers between devices: 125 us -> 137 us
    unnamed x1 -> x0, other arithmetic: 34.3 us -> none
    all_to_all x1, waiting for transfers between devices: 15.1 us -> 26.4 us  [sum_in_two_steps(): lax.all_to_all(nearer, far, split_axis=0, concat_axis=0, tiled=True)]
    reshape x1 -> x0, local copies, waits for them, and re-layouts: 5.62 us -> none  [per_device(): grad_columns.reshape(1, replica_count * local_rows, group_count * slab_rows)]
    all_to_all x1, local copies, waits for them, and re-layouts: 6.77 us -> 2.29 us  [per_device(): lax.all_to_all(jnp.stack(jnp.split(grad_columns.reshape(1, replica_count...]
    unnamed x22 -> x25, local copies, waits for them, and re-layouts: 17.7 us -> 13.4 us
  transfers between devices with their start and end apart: 6 -> 6, of which waited for: 5 -> 5; matrix products, arithmetic and copies ran while one was open for 42% -> 33% of each run, Pallas kernels for 0% -> 0%
where the time goes in v1:
time: 363 us; the launch traced here: 361 us
  waiting for transfers between devices  137 us (38%)
  matrix products  71.5 us (20%)
  local copies, waits for them, and re-layouts  67.7 us (19%)
  starting transfers between devices  34.3 us (9%)
  other arithmetic  19 us (5%)
  blocking collectives  18 us (5%)
  between operations  14.2 us (4%)
    all_gather x1, waiting for transfers between devices, per_device(): all_output = lax.all_gather(output_flat, 'rep', axis=0, tiled=True)  77.7 us
    all_to_all x1, waiting for transfers between devices, sum_in_two_steps(): lax.all_to_all(nearer, far, split_axis=0, concat_axis=0, tiled=True)  26.4 us
    all_to_all x2, waiting for transfers between devices, from_everyone(): lax.all_to_all(jnp.broadcast_to(value[None], (count, *value.shape)), axis...  17.3 us
    all_to_all x1, waiting for transfers between devices, per_device(): lax.all_to_all(jnp.stack(jnp.split(grad_columns.reshape(1, replica_count...  14.6 us
    dot_general x1, matrix products, per_device(): jnp.einsum('rlp,rle->rpe', gathered_ctx, output_blocks, preferred_element...  13.9 us
    all_to_all x2, starting transfers between devices, from_everyone(): lax.all_to_all(jnp.broadcast_to(value[None], (count, *value.shape)), axis...  13.6 us
    unnamed x25, local copies, waits for them, and re-layouts  13.4 us
    reduce_sum x1, other arithmetic, per_device(): jnp.sum(lax.optimization_barrier(device_terms).astype(jnp.float32), axis=0)  12.8 us
  transfers between devices with their start and end apart: 6, of which 5 were waited for; matrix products, arithmetic and copies ran while one was open for 33% of the time, Pallas kernels for 0%

profile of v1, /device:TPU:4, one launch (start us, length us, event | category | flops | bytes accessed | tf_op | source)
XLA Modules:
  0.0 361.4 jit_solution(6261090021535119067)
XLA Ops:
  7.2 0.0 copy-start
  7.2 0.0 all-gather.3.cloned.1.call-start
  7.2 0.7 all-gather.3.cloned.1.call-update
  7.9 0.8 dynamic-slice_convert_fusion
  8.7 0.6 broadcast_in_dim.52
  9.3 9.2 %all-to-all-start.2 = ((bf16[16,12,12]{1,2,0:T(8,128)(2,1)}), bf16[16,12,12]{1,2,0:T(8,128)(2,1)S(1)}, u32[]{:S(2)}, u32[]{:S(2)}) async-start(bf16[16,12,12]{1,2,0:T(8,128)(2,1)} %broadcast_in_dim.52), calls=%async_computation.2 | async-start | bytes 131072 | tf_op jit(solution)/shard_map/all_to_all | solution.py:14
  18.6 9.0 %all-to-all-done.2 = bf16[16,12,12]{1,2,0:T(8,128)(2,1)S(1)} async-done(((bf16[16,12,12]{1,2,0:T(8,128)(2,1)}), bf16[16,12,12]{1,2,0:T(8,128)(2,1)S(1)}, u32[]{:S(2)}, u32[]{:S(2)}) %all-to-all-start.2) | async-done | bytes 4640 | tf_op jit(solution)/shard_map/all_to_all | solution.py:14
  27.6 0.2 reshape.101
  27.8 3.7 %all_to_all.44 = bf16[2,2,1152]{2,1,0:T(2,128)(2,1)S(1)} all-to-all(bf16[2,2,1152]{2,1,0:T(2,128)(2,1)S(1)} %reshape.101), channel_id=1, replica_groups=mesh['group_0'=8,'group_1'=2,'group_2'=2,'rep'=8] {'group_2'}, dimensions={0} | all-to-all | bytes 18432 | tf_op jit(solution)/shard_map/all_to_all | solution.py:14
  31.5 1.3 broadcast_in_dim.50
  32.8 4.4 %all-to-all-start = ((bf16[16,12,3072]{2,1,0:T(8,128)(2,1)}), bf16[16,12,3072]{2,1,0:T(8,128)(2,1)}, u32[]{:S(2)}, u32[]{:S(2)}) async-start(bf16[16,12,3072]{2,1,0:T(8,128)(2,1)} %broadcast_in_dim.50), calls=%async_computation | async-start | bytes 3145728 | tf_op jit(solution)/shard_map/all_to_all | solution.py:14
  37.3 1.6 copy.123
  38.9 2.6 copy.122
  41.5 1.7 copy.124
  43.2 7.4 %fusion.51 = (f32[24,256]{1,0:T(8,128)S(1)}, f32[24,256,256]{1,2,0:T(8,128)}) fusion(bf16[256,24,128]{0,2,1:T(8,128)(2,1)} %bitcast.99, bf16[256,24,128]{0,2,1:T(8,128)(2,1)} %bitcast.101), kind=kOutput, calls=%fused_computation.54 | convolution fusion | flops 407372032 | bytes 9461760 | tf_op jit(solution)/shard_map/while/body/eval_jaxpr/sub | solution.py:70
  50.6 4.6 %fusion.33 = bf16[256,24,128]{0,2,1:T(8,128)(2,1)} fusion(bf16[256,24,128]{0,2,1:T(8,128)(2,1)S(1)} %bitcast.95, f32[24,256,256]{1,2,0:T(8,128)} %get-tuple-element.70, f32[24,256]{1,0:T(8,128)S(1)} %get-tuple-element.69), kind=kOutput, calls=%fused_computation.28 | convolution fusion | flops 406585344 | bytes 9461760 | tf_op jit(solution)/shard_map/while/body/eval_jaxpr/hqk,khd->qhd/dot_general | solution.py:73
  55.2 2.4 reshape_reshape.12
  57.5 0.7 copy.110
  58.2 1.5 copy.111
  59.7 0.2 reshape.102
  60.0 0.2 copy.97
  60.1 0.3 reshape.98
  60.4 2.4 mul.32
  62.8 6.1 %copy.98 = f32[384,3072]{1,0:T(8,128)} copy(f32[384,3072]{0,1:T(8,128)} %bitcast.92) | data formatting | bytes 9437184 | tf_op jit(solution)/shard_map/mul | solution.py:54
  68.9 8.3 %all-to-all-done = bf16[16,12,3072]{2,1,0:T(8,128)(2,1)} async-done(((bf16[16,12,3072]{2,1,0:T(8,128)(2,1)}), bf16[16,12,3072]{2,1,0:T(8,128)(2,1)}, u32[]{:S(2)}, u32[]{:S(2)}) %all-to-all-start) | async-done | bytes 1179680 | tf_op jit(solution)/shard_map/all_to_all | solution.py:14
  77.2 2.1 copy.94
  79.3 0.3 broadcast_in_dim.51
  79.6 5.6 %all_to_all.45 = bf16[2,16,12,3072]{3,1,2,0:T(8,128)(2,1)S(1)} all-to-all(bf16[2,16,12,3072]{3,1,2,0:T(8,128)(2,1)S(1)} %broadcast_in_dim.51), channel_id=1, replica_groups=mesh['group_0'=8,'group_1'=2,'group_2'=2,'rep'=8] {'group_2'}, dimensions={0} | all-to-all | bytes 4718592 | tf_op jit(solution)/shard_map/all_to_all | solution.py:14
  85.2 7.4 %all-to-all-start.5 = ((bf16[8,256,384]{1,2,0:T(8,128)(2,1)}), bf16[8,256,384]{1,2,0:T(8,128)(2,1)}, u32[]{:S(2)}, u32[]{:S(2)}) async-start(bf16[8,256,384]{1,2,0:T(8,128)(2,1)} %copy.111), calls=%async_computation.5 | async-start | bytes 3145728 | tf_op jit(solution)/shard_map/all_to_all | solution.py:121
  92.6 0.6 convert_bitcast_fusion
  93.2 5.5 %copy.95 = f32[16,2,12,3072]{3,2,1,0:T(8,128)} copy(f32[16,2,12,3072]{3,0,2,1:T(8,128)S(1)} %convert_bitcast_fusion) | data formatting | bytes 9437184 | tf_op jit(solution)/shard_map/convert_element_type | solution.py:54
  98.7 5.4 %reshape.97 = f32[384,3072]{1,0:T(8,128)} reshape(f32[16,2,12,3072]{3,2,1,0:T(8,128)} %copy.95) | data formatting | bytes 9437184 | tf_op jit(solution)/shard_map/convert_element_type | solution.py:54
  104.1 77.7 %all-gather.3.cloned.1.call-done = bf16[1,2048,3072]{2,1,0:T(8,128)(2,1)} async-done(((bf16[1,256,3072]{2,1,0:T(8,128)(2,1)}), bf16[1,2048,3072]{2,1,0:T(8,128)(2,1)}) %all-gather.3.cloned.1.call-update) | async-done | bytes 12582928 | tf_op jit(solution)/shard_map/all_gather | solution.py:116
  181.8 10.8 %fusion.22 = bf16[1,2048,384]{1,2,0:T(8,128)(2,1)S(1)} fusion(bf16[1,2048,3072]{2,1,0:T(8,128)(2,1)} %all-gather.3.cloned.1.call-done, f32[384,3072]{1,0:T(8,128)} %reshape.97, f32[384,3072]{1,0:T(8,128)} %copy.98), kind=kOutput, calls=%fused_computation.21 | convolution fusion | flops 4834983936 | bytes 23592960 | tf_op jit(solution)/shard_map/dot_general | solution.py:123
  192.6 0.7 fusion.45
  193.3 0.7 fusion.44
  194.0 0.7 fusion.43
  194.7 0.7 fusion.42
  195.4 0.7 fusion.41
  196.1 0.7 fusion.40
  196.8 0.7 fusion.39
  197.5 0.7 fusion.38
  198.2 13.9 %convolution_convert_fusion = bf16[8,384,3072]{2,1,0:T(8,128)(2,1)} fusion(bf16[8,256,384]{1,2,0:T(8,128)(2,1)} %all-to-all-done.5, bf16[8,256,3072]{2,1,0:T(8,128)(2,1)} %bitcast.93), kind=kOutput, calls=%fused_computation.5 | convolution fusion | flops 4841275392 | bytes 33030144 | tf_op jit(solution)/shard_map/rlp,rle->rpe/dot_general | solution.py:134
  212.2 12.8 %convert_reduce_fusion = f32[384,3072]{1,0:T(8,128)} fusion(bf16[8,384,3072]{2,1,0:T(8,128)(2,1)} %convolution_convert_fusion), kind=kLoop, calls=%fused_computation.2 | loop fusion | flops 17694720 | bytes 23592960 | tf_op jit(solution)/shard_map/reduce_sum | solution.py:138
  224.9 5.5 %reshape_reshape.13 = f32[16,2,12,3072]{3,2,1,0:T(8,128)} reshape(f32[384,3072]{1,0:T(8,128)} %convert_reduce_fusion) | data formatting | bytes 9437184 | tf_op jit(solution)/shard_map/reshape;reshape | solution.py:33
  230.5 5.5 %copy.112 = f32[2,16,12,3072]{3,1,2,0:T(8,128)S(1)} copy(f32[2,16,12,3072]{3,2,0,1:T(8,128)} %bitcast.91) | data formatting | bytes 9437184 | tf_op jit(solution)/shard_map/transpose | solution.py:33
  236.0 8.6 %all_to_all.46 = f32[2,16,12,3072]{3,1,2,0:T(8,128)} all-to-all(f32[2,16,12,3072]{3,1,2,0:T(8,128)S(1)} %copy.112), channel_id=1, replica_groups=mesh['group_0'=8,'group_1'=2,'group_2'=2,'rep'=8] {'group_2'}, dimensions={0} | all-to-all | bytes 9437184 | tf_op jit(solution)/shard_map/all_to_all | solution.py:38
  244.6 6.9 %all-to-all-start.4 = ((bf16[8,1,256,384]{2,3,1,0:T(8,128)(2,1)}), bf16[8,1,256,384]{2,3,1,0:T(8,128)(2,1)}, u32[]{:S(2)}, u32[]{:S(2)}) async-start(bf16[8,1,256,384]{2,3,1,0:T(8,128)(2,1)} %fusion.38), calls=%async_computation.4 | async-start | bytes 3145728 | tf_op jit(solution)/shard_map/all_to_all | solution.py:143
  251.5 2.9 reduce_sum.50
  254.4 3.0 copy.113
  257.4 14.6 %all-to-all-done.4 = bf16[8,1,256,384]{2,3,1,0:T(8,128)(2,1)} async-done(((bf16[8,1,256,384]{2,3,1,0:T(8,128)(2,1)}), bf16[8,1,256,384]{2,3,1,0:T(8,128)(2,1)}, u32[]{:S(2)}, u32[]{:S(2)}) %all-to-all-start.4) | async-done | bytes 1572896 | tf_op jit(solution)/shard_map/all_to_all | solution.py:143
  272.1 6.4 %all-to-all-start.7 = ((f32[16,12,3072]{2,1,0:T(8,128)}), f32[16,12,3072]{2,1,0:T(8,128)}, u32[]{:S(2)}, u32[]{:S(2)}) async-start(f32[16,12,3072]{2,1,0:T(8,128)} %copy.113), calls=%async_computation.7 | async-start | bytes 6291456 | tf_op jit(solution)/shard_map/all_to_all | solution.py:46
  278.4 2.3 copy.99
  280.7 0.5 copy.100
  281.2 1.3 reshape.93
  282.6 5.6 %convolution_convert_fusion.2 = bf16[24,128,256]{2,1,0:T(8,128)(2,1)} fusion(bf16[256,24,128]{0,2,1:T(8,128)(2,1)} %reshape.93, f32[24,256,256]{1,2,0:T(8,128)} %get-tuple-element.70, f32[24,256]{1,0:T(8,128)S(1)} %get-tuple-element.69), kind=kOutput, calls=%fused_computation.25 | convolution fusion | flops 406585344 | bytes 9461760 | tf_op jit(solution)/shard_map/while/body/eval_jaxpr/hqk,qhd->khd/dot_general | solution.py:88
  288.2 2.7 copy.116
  290.9 5.1 %fusion.52 = f32[24,256,256]{1,2,0:T(8,128)} fusion(bf16[256,24,128]{0,2,1:T(8,128)(2,1)} %bitcast.96, bf16[256,24,128]{0,2,1:T(8,128)(2,1)S(1)} %copy-done.2), kind=kOutput, calls=%fused_computation.56 | convolution fusion | flops 402653184 | bytes 9437184 | tf_op jit(solution)/shard_map/while/body/eval_jaxpr/qhd,khd->hqk/dot_general | solution.py:91
  296.0 12.2 %fusion.25 = bf16[24,256,128]{1,2,0:T(8,128)(2,1)} fusion(bf16[256,24,128]{0,2,1:T(8,128)(2,1)} %bitcast.102, f32[24,256,256]{1,2,0:T(8,128)} %fusion.52, f32[24,256,256]{1,2,0:T(8,128)} %get-tuple-element.70, f32[24,256]{1,0:T(8,128)S(1)} %get-tuple-element.69), kind=kOutput, calls=%fused_computation.22 | convolution fusion | flops 414456064 | bytes 15753216 | tf_op jit(solution)/shard_map/while/body/eval_jaxpr/hqk,khd->qhd/dot_general | solution.py:94
  308.2 2.7 copy.114
  310.9 11.9 %fusion.28 = bf16[24,256,128]{1,2,0:T(8,128)(2,1)} fusion(bf16[256,24,128]{0,2,1:T(8,128)(2,1)S(1)} %bitcast.100, f32[24,256,256]{1,2,0:T(8,128)} %fusion.52, f32[24,256,256]{1,2,0:T(8,128)} %get-tuple-element.70, f32[24,256]{1,0:T(8,128)S(1)} %get-tuple-element.69), kind=kOutput, calls=%fused_computation.23 | convolution fusion | flops 414456064 | bytes 15753216 | tf_op jit(solution)/shard_map/while/body/eval_jaxpr/hqk,qhd->khd/dot_general | solution.py:95
  322.8 2.6 copy.115
  325.4 26.4 %all-to-all-done.7 = f32[16,12,3072]{2,1,0:T(8,128)} async-done(((f32[16,12,3072]{2,1,0:T(8,128)}), f32[16,12,3072]{2,1,0:T(8,128)}, u32[]{:S(2)}, u32[]{:S(2)}) %all-to-all-start.7) | async-done | bytes 2359328 | tf_op jit(solution)/shard_map/all_to_all | solution.py:46
  351.8 2.8 reduce_sum.51
  (16 shorter events, 0.1 us)
Async XLA Ops:
  7.2 11.4 %copy-start = (bf16[96,3072]{1,0:T(8,128)(2,1)S(1)}, bf16[96,3072]{1,0:T(8,128)(2,1)}, u32[]{:S(2)}) copy-start(bf16[96,3072]{1,0:T(8,128)(2,1)} %param.10) | copy-start | bytes 1769476
  7.2 174.6 %all-gather.3.cloned.1.call-start = ((), (), s32[]{:S(2)}) async-start(), calls=%async_computation.8 | async-start | bytes 14155776 | tf_op jit(solution)/shard_map/all_gather | solution.py:116
  9.3 18.3 %all-to-all-start.2 = ((bf16[16,12,12]{1,2,0:T(8,128)(2,1)}), bf16[16,12,12]{1,2,0:T(8,128)(2,1)S(1)}, u32[]{:S(2)}, u32[]{:S(2)}) async-start(bf16[16,12,12]{1,2,0:T(8,128)(2,1)} %broadcast_in_dim.52), calls=%async_computation.2 | async-start | bytes 131072 | tf_op jit(solution)/shard_map/all_to_all | solution.py:14
  31.5 5.7 %copy-start.4 = (bf16[1,256,3072]{2,1,0:T(8,128)(2,1)S(1)}, bf16[1,256,3072]{2,1,0:T(8,128)(2,1)}, u32[]{:S(2)}) copy-start(bf16[1,256,3072]{2,1,0:T(8,128)(2,1)} %param.6) | copy-start | bytes 4718596
  32.8 44.4 %all-to-all-start = ((bf16[16,12,3072]{2,1,0:T(8,128)(2,1)}), bf16[16,12,3072]{2,1,0:T(8,128)(2,1)}, u32[]{:S(2)}, u32[]{:S(2)}) async-start(bf16[16,12,3072]{2,1,0:T(8,128)(2,1)} %broadcast_in_dim.50), calls=%async_computation | async-start | bytes 3145728 | tf_op jit(solution)/shard_map/all_to_all | solution.py:14
  43.2 7.4 %copy-start.3 = (bf16[1,256,3072]{1,2,0:T(8,128)(2,1)}, bf16[1,256,3072]{1,2,0:T(8,128)(2,1)S(1)}, u32[]{:S(2)}) copy-start(bf16[1,256,3072]{1,2,0:T(8,128)(2,1)S(1)} %copy.124) | copy-start | bytes 4718596
  85.2 113.0 %all-to-all-start.5 = ((bf16[8,256,384]{1,2,0:T(8,128)(2,1)}), bf16[8,256,384]{1,2,0:T(8,128)(2,1)}, u32[]{:S(2)}, u32[]{:S(2)}) async-start(bf16[8,256,384]{1,2,0:T(8,128)(2,1)} %copy.111), calls=%async_computation.5 | async-start | bytes 3145728 | tf_op jit(solution)/shard_map/all_to_all | solution.py:121
  244.6 27.5 %all-to-all-start.4 = ((bf16[8,1,256,384]{2,3,1,0:T(8,128)(2,1)}), bf16[8,1,256,384]{2,3,1,0:T(8,128)(2,1)}, u32[]{:S(2)}, u32[]{:S(2)}) async-start(bf16[8,1,256,384]{2,3,1,0:T(8,128)(2,1)} %fusion.38), calls=%async_computation.4 | async-start | bytes 3145728 | tf_op jit(solution)/shard_map/all_to_all | solution.py:143
  272.1 79.7 %all-to-all-start.7 = ((f32[16,12,3072]{2,1,0:T(8,128)}), f32[16,12,3072]{2,1,0:T(8,128)}, u32[]{:S(2)}, u32[]{:S(2)}) async-start(f32[16,12,3072]{2,1,0:T(8,128)} %copy.113), calls=%async_computation.7 | async-start | bytes 6291456 | tf_op jit(solution)/shard_map/all_to_all | solution.py:46
  288.2 2.7 copy-start.2
  308.2 2.7 copy-start.5
  322.7 31.8 %copy-start.1 = (bf16[96,3072]{1,0:T(8,128)(2,1)S(1)}, bf16[96,3072]{1,0:T(8,128)(2,1)}, u32[]{:S(2)}) copy-start(bf16[96,3072]{1,0:T(8,128)(2,1)} %param.10) | copy-start | bytes 1769476
Sparse Core Ops, SparseCore 0:
  10.6 171.1 all-gather.2
